TPU v7x, 32 devices: a whole 2x2x4 slice. The times are simulated.
32 devices in a mesh: ctx: 16 (over z, y, core), tp: 2 (over x).
Axes of the slice: x: 2, y: 2, z: 4, core: 2. Of those that a mesh axis runs over, the one named last changes fastest.
Arguments:
- query: bfloat16 [2048, 4096], P('ctx', 'tp'), may hold values from -6 to 6
- key_in: bfloat16 [2048, 4096], P('ctx', 'tp'), may hold values from -6 to 6
- value: bfloat16 [2048, 4096], P('ctx', 'tp'), may hold values from -6 to 6
- short_taps: float32 [3, 3, 4096], P(None, None, 'tp'), may hold values from -3.5 to 3.5
- skip_gain: float32 [4096], P('tp'), may hold values from -1 to 1
- filter_spectrum: float32 [2048, 2, 2, 4096], P('ctx', None, None, 'tp'), may hold values from -6 to 6
- out_weight: bfloat16 [4096, 4096], P('tp'), may hold values from -0.09375 to 0.09375
Outputs:
- mixed_out: bfloat16 [2048, 4096], P('ctx', 'tp')
All inputs are finite; a program needn't handle non-finite values.
Results may differ from a plain program's by a relative error of at most 0.0049.
Values may be sent and summed in bfloat16 or wider, within the bound.
No kernel may reach another device: no remote copies, remote signals or barrier semaphores. Data moves between devices by JAX's collectives and lax.ppermute only.
A program may use at most 128 MiB of HBM per device.

v0:
```python
import functools
import math

import jax
import jax.numpy as jnp
from jax import lax
from jax.experimental import pallas as pl
from jax.experimental.pallas import tpu as pltpu
from jax.sharding import PartitionSpec as P


RADIX = 8
ROWS = 16
LANES = 128
FAR_CHUNKS = (768, 1280)
STEP = 256
GROUP = 128
EDGE = 8


def shifted_in(rows, axis):
    count = lax.axis_size(axis)
    return lax.ppermute(rows, axis, [(i, i + 1) for i in range(count - 1)])


def causal_filter(signal, tail, taps):
    values = jnp.concatenate([tail, signal], axis=0).astype(jnp.float32)
    return taps[0] * values[2:] + taps[1] * values[1:-1] + taps[2] * values[:-2]


def turn(rows, columns, order):
    index = rows[:, None] * columns[None, :] % order
    angle = (2.0 * math.pi / order) * index.astype(jnp.float32)
    return jnp.cos(angle), jnp.sin(angle)


def exact_dot(left, right):
    return jnp.dot(left, right, precision=lax.Precision.HIGHEST, preferred_element_type=jnp.float32)


def radix_of(order):
    return 2 ** ((order.bit_length() - 1) // 2)


def long_filter(signal, spectrum_real, spectrum_imag):
    length, width = signal.shape
    order = spectrum_real.shape[0]
    radix = radix_of(order)
    span, depth = order // radix, length // radix
    low = jnp.arange(span, dtype=jnp.int32)
    deep = jnp.arange(depth, dtype=jnp.int32)
    lanes = jnp.arange(radix, dtype=jnp.int32)
    inner_cos, inner_sin = turn(low, deep, span)
    twiddle_cos, twiddle_sin = (t[:, :, None] for t in turn(lanes, low, order))
    outer_cos, outer_sin = turn(lanes, lanes, radix)

    samples = signal.astype(jnp.float32).reshape(depth, radix * width)
    real = exact_dot(inner_cos, samples).reshape(span, radix, width).transpose(1, 0, 2)
    imag = -exact_dot(inner_sin, samples).reshape(span, radix, width).transpose(1, 0, 2)
    real, imag = (
        (real * twiddle_cos + imag * twiddle_sin).reshape(radix, span * width),
        (imag * twiddle_cos - real * twiddle_sin).reshape(radix, span * width),
    )
    real, imag = (
        exact_dot(outer_cos, real) + exact_dot(outer_sin, imag),
        exact_dot(outer_cos, imag) - exact_dot(outer_sin, real),
    )
    spectrum_real = spectrum_real.astype(jnp.float32).reshape(radix, span * width)
    spectrum_imag = spectrum_imag.astype(jnp.float32).reshape(radix, span * width)
    real, imag = (
        real * spectrum_real - imag * spectrum_imag,
        real * spectrum_imag + imag * spectrum_real,
    )
    real, imag = (
        (exact_dot(outer_cos, real) - exact_dot(outer_sin, imag)).reshape(radix, span, width),
        (exact_dot(outer_cos, imag) + exact_dot(outer_sin, real)).reshape(radix, span, width),
    )
    real, imag = (
        (real * twiddle_cos - imag * twiddle_sin).transpose(1, 0, 2).reshape(span, radix * width),
        (imag * twiddle_cos + real * twiddle_sin).transpose(1, 0, 2).reshape(span, radix * width),
    )
    result = exact_dot(inner_cos.T, real) - exact_dot(inner_sin.T, imag)
    return (result / order).reshape(length, width)


def split(value):
    high = value.astype(jnp.bfloat16)
    return high, (value - high.astype(jnp.float32)).astype(jnp.bfloat16)


def filtered_block(signal_ref, tails_ref, taps_ref, which, lanes):
    values = signal_ref[:, lanes].astype(jnp.float32)
    tails = tails_ref[:, lanes].astype(jnp.float32)
    older, newer = tails[2 * which : 2 * which + 1], tails[2 * which + 1 : 2 * which + 2]
    row = lax.broadcasted_iota(jnp.int32, values.shape, 0)
    one_back = jnp.where(row == 0, newer, pltpu.roll(values, 1, 0))
    two_back = jnp.where(row == 0, older, jnp.where(row == 1, newer, pltpu.roll(values, 2, 0)))
    taps = taps_ref[which, :, lanes]
    return taps[0:1] * values + taps[1:2] * one_back + taps[2:3] * two_back


def tails_kernel(query_ref, key_ref, value_ref, tails_ref):
    rows = query_ref.shape[0]
    for which, ref in enumerate((query_ref, key_ref, value_ref)):
        tails_ref[2 * which : 2 * which + 2, :] = ref[...].astype(jnp.float32)[rows - 2 :].astype(jnp.bfloat16)


def own_tails(query, key_in, value):
    tokens, channels = query.shape
    last = pl.BlockSpec((ROWS, channels), lambda i: (tokens // ROWS - 1, 0))
    return pl.pallas_call(
        tails_kernel,
        grid=(1,),
        out_shape=jax.ShapeDtypeStruct((6, channels), query.dtype),
        in_specs=[last] * 3,
        out_specs=pl.BlockSpec((6, channels), lambda i: (0, 0)),
        compiler_params=pltpu.CompilerParams(vmem_limit_bytes=4 * 2**20),
    )(*(pltpu.with_memory_space_constraint(a, pltpu.HBM) for a in (query, key_in, value)))


def gather_rows(size, count, invert=False):
    row = lax.broadcasted_iota(jnp.int32, (size, size), 0)
    column = lax.broadcasted_iota(jnp.int32, (size, size), 1)
    if invert:
        row, column = column, row
    inner = size // count
    match = column == (row % inner) * count + row // inner
    return jnp.where(match, 1.0, 0.0).astype(jnp.bfloat16)


def exact_rows(matrix, left, right):
    both = jnp.concatenate([left, right], axis=1)
    return jnp.dot(matrix, both, preferred_element_type=jnp.float32).astype(jnp.bfloat16)


def unshifted(values, taps):
    return taps[0:1] * values + taps[1:2] * pltpu.roll(values, 1, 0) + taps[2:3] * pltpu.roll(values, 2, 0)


def prepare_kernel(spectrum_ref, key_ref, value_ref, taps_ref, sent_ref, *scratch):
    spectrum, key, value, taps, staged, in_sems, out_sems = scratch
    devices, _, block = staged.shape
    tokens = key.shape[0]
    fine = 2 * devices
    slab = GROUP * fine
    groups = spectrum.shape[0] // slab
    loads = [
        pltpu.make_async_copy(source, target, in_sems.at[i])
        for i, (source, target) in enumerate(((taps_ref, taps), (key_ref, key), (value_ref, value)))
    ] + [
        pltpu.make_async_copy(
            spectrum_ref.at[pl.ds(g * slab, slab)], spectrum.at[pl.ds(g * slab, slab)], in_sems.at[3 + g]
        )
        for g in range(groups)
    ]
    for load in loads:
        load.start()
    stores = []

    def store(start, size):
        rows = pl.ds(start, size)
        stores.append(
            pltpu.make_async_copy(staged.at[:, rows], sent_ref.at[:, rows], out_sems.at[len(stores)])
        )
        stores[-1].start()

    for load in loads[:3]:
        load.wait()
    edge = tokens + 2 * GROUP * groups
    for j in range(devices):
        lanes = pl.ds(j * block, block)
        k, v = key[:, lanes].astype(jnp.float32), value[:, lanes].astype(jnp.float32)
        mixed = unshifted(k, taps[1, :, lanes]) * unshifted(v, taps[2, :, lanes])
        staged[j, pl.ds(0, tokens), :] = mixed.astype(jnp.bfloat16)
        ends = jnp.concatenate([k[:2], v[:2], k[tokens - 2 :], v[tokens - 2 :]], axis=0)
        staged[j, pl.ds(edge, EDGE), :] = ends.astype(jnp.bfloat16)
    store(0, tokens)
    store(edge, EDGE)

    matrix = gather_rows(EDGE * fine, fine)
    for g in range(groups):
        loads[3 + g].wait()
        start = tokens + 2 * GROUP * g
        for h in range(0, GROUP, 2 * EDGE):
            slabs = [
                spectrum[pl.ds((g * GROUP + h + p) * fine, EDGE * fine), :].astype(jnp.bfloat16)
                for p in (0, EDGE)
            ]
            both = exact_rows(matrix, *slabs)
            for s in range(fine):
                rows = both[s * EDGE : (s + 1) * EDGE]
                pair = jnp.concatenate([rows[:, :block], rows[:, block:]], axis=0)
                staged[s // 2, pl.ds(start + s % 2 * GROUP + h, 2 * EDGE), :] = pair
        store(start, 2 * GROUP)
    for copy in stores:
        copy.wait()


def prepared(key_in, value, short_taps, filter_spectrum, devices):
    tokens, _, _, channels = filter_spectrum.shape
    block, pairs = channels // devices, 2 * tokens
    groups = pairs // GROUP
    view = (
        filter_spectrum.reshape(tokens, 2, 2, devices, block)
        .transpose(0, 1, 3, 2, 4)
        .reshape(2 * pairs * devices, block)
    )
    rows = tokens + 2 * pairs + EDGE
    remote = pl.BlockSpec(memory_space=pltpu.HBM)
    inputs = [
        pltpu.with_memory_space_constraint(a, pltpu.HBM) for a in (view, key_in, value, short_taps)
    ]
    return pl.pallas_call(
        prepare_kernel,
        out_shape=pltpu.HBM((devices, rows, block), jnp.bfloat16),
        in_specs=[remote] * 4,
        out_specs=remote,
        scratch_shapes=[
            pltpu.VMEM(view.shape, jnp.float32),
            pltpu.VMEM((tokens, channels), jnp.bfloat16),
            pltpu.VMEM((tokens, channels), jnp.bfloat16),
            pltpu.VMEM(short_taps.shape, jnp.float32),
            pltpu.VMEM((devices, rows, block), jnp.bfloat16),
            pltpu.SemaphoreType.DMA((3 + groups,)),
            pltpu.SemaphoreType.DMA((2 + groups,)),
        ],
        compiler_params=pltpu.CompilerParams(vmem_limit_bytes=20 * 2**20),
        cost_estimate=pl.CostEstimate(flops=0, bytes_accessed=view.size * 6, transcendentals=0),
    )(*inputs)


def gate_kernel(tails_ref, *refs):
    sources, (gate_ref, direct_ref), held, sems = refs[:5], refs[5:7], refs[7:12], refs[12]
    query_ref, key_ref, value_ref, taps_ref, gain_ref = held
    loads = [
        pltpu.make_async_copy(source, target, sems.at[i])
        for i, (source, target) in enumerate(zip(sources, held))
    ]
    for load in loads:
        load.start()
    for load in loads:
        load.wait()
    _, channels = query_ref.shape
    for j in range(channels // LANES):
        lanes = pl.ds(j * LANES, LANES)
        mixed = filtered_block(key_ref, tails_ref, taps_ref, 1, lanes) * filtered_block(
            value_ref, tails_ref, taps_ref, 2, lanes
        )
        gate_ref[:, lanes] = filtered_block(query_ref, tails_ref, taps_ref, 0, lanes)
        direct_ref[:, lanes] = gain_ref[:, lanes] * mixed


def gates(query, key_in, value, tails, short_taps, skip_gain):
    shape = jax.ShapeDtypeStruct(query.shape, jnp.float32)
    whole, remote = pl.BlockSpec(memory_space=pltpu.VMEM), pl.BlockSpec(memory_space=pltpu.HBM)
    inputs = [query, key_in, value, short_taps, skip_gain[None, :]]
    return pl.pallas_call(
        gate_kernel,
        out_shape=(shape, shape),
        in_specs=[whole] + [remote] * len(inputs),
        out_specs=(whole, whole),
        scratch_shapes=[
            *(pltpu.VMEM(a.shape, a.dtype) for a in inputs),
            pltpu.SemaphoreType.DMA((len(inputs),)),
        ],
        compiler_params=pltpu.CompilerParams(vmem_limit_bytes=16 * 2**20),
        cost_estimate=pl.CostEstimate(
            flops=20 * query.size, bytes_accessed=14 * query.size, transcendentals=0
        ),
    )(tails, *(pltpu.with_memory_space_constraint(a, pltpu.HBM) for a in inputs))


def column_copies(weight_ref, held, sems, first):
    chunks, _, width = held.shape
    return [
        pltpu.make_async_copy(
            weight_ref.at[:, pl.ds(pl.multiple_of(first + i * width, LANES), width)],
            held.at[i],
            sems.at[i],
        )
        for i in range(chunks)
    ]


def multiply(gated_ref, share_ref, held, copies):
    width = held.shape[2]
    for i, copy in enumerate(copies):
        copy.wait()
        share_ref[:, pl.ds(i * width, width)] = jnp.dot(
            gated_ref[...], held[i], preferred_element_type=jnp.float32
        ).astype(share_ref.dtype)


def gated_kernel(conv_ref, gate_ref, direct_ref, weight_ref, gated_ref, share_ref, held, sems):
    devices, _, block = conv_ref.shape
    columns = weight_ref.shape[1] // 2
    copies = column_copies(weight_ref, held, sems, (1 - lax.axis_index("tp")) * columns)
    for copy in copies:
        copy.start()
    for j in range(devices):
        lanes = pl.ds(j * block, block)
        gated_ref[:, lanes] = (
            gate_ref[:, lanes] * (conv_ref[j].astype(jnp.float32) + direct_ref[:, lanes])
        ).astype(jnp.bfloat16)
    multiply(gated_ref, share_ref, held, copies)


def share_kernel(far, offset, gated_ref, weight_ref, share_ref, held, sems):
    columns = weight_ref.shape[1] // 2
    rank = lax.axis_index("tp")
    copies = column_copies(weight_ref, held, sems, (1 - rank if far else rank) * columns + offset)
    for copy in copies:
        copy.start()
    multiply(gated_ref, share_ref, held, copies)


def projected(convolved, gate_signal, direct, out_weight):
    tokens, channels = gate_signal.shape
    columns = out_weight.shape[1] // 2
    whole, remote = pl.BlockSpec(memory_space=pltpu.VMEM), pl.BlockSpec(memory_space=pltpu.HBM)
    out_weight = pltpu.with_memory_space_constraint(out_weight, pltpu.HBM)

    def share(kernel, operands, extra, width, step, dtype):
        return pl.pallas_call(
            kernel,
            out_shape=(*extra, jax.ShapeDtypeStruct((tokens, width), dtype)),
            in_specs=[whole] * len(operands) + [remote],
            out_specs=(whole,) * (len(extra) + 1),
            scratch_shapes=[
                pltpu.VMEM((width // step, channels, step), jnp.bfloat16),
                pltpu.SemaphoreType.DMA((width // step,)),
            ],
            compiler_params=pltpu.CompilerParams(vmem_limit_bytes=20 * 2**20),
            cost_estimate=pl.CostEstimate(
                flops=2 * tokens * channels * width, bytes_accessed=2 * channels * width, transcendentals=0
            ),
        )(*operands, out_weight)

    swap = [(0, 1), (1, 0)]
    widths = FAR_CHUNKS if sum(FAR_CHUNKS) == columns else (columns,)
    arrived, offset, gated = [], 0, None
    for width in widths:
        if gated is None:
            gated, far = share(
                gated_kernel,
                (convolved, gate_signal, direct),
                (jax.ShapeDtypeStruct((tokens, channels), jnp.bfloat16),),
                width,
                STEP,
                jnp.bfloat16,
            )
        else:
            kernel = functools.partial(share_kernel, True, offset)
            (far,) = share(kernel, (gated,), (), width, STEP, jnp.bfloat16)
        arrived.append(lax.ppermute(far, "tp", swap))
        offset += width
    kernel = functools.partial(share_kernel, False, 0)
    (near,) = share(kernel, (gated,), (), columns, 2 * STEP, jnp.float32)
    return (near + jnp.concatenate(arrived, axis=1).astype(jnp.float32)).astype(jnp.bfloat16)


def butterfly(parts, sign):
    count = len(parts)
    if count == 1:
        return parts
    even, odd = butterfly(parts[0::2], sign), butterfly(parts[1::2], sign)
    half = count // 2
    low, high = [], []
    for j in range(half):
        real, imag = odd[j]
        if 4 * j == count:
            real, imag = (-imag, real) if sign > 0 else (imag, -real)
        elif j:
            c, s = math.cos(2.0 * math.pi * j / count), sign * math.sin(2.0 * math.pi * j / count)
            if 8 * j == count:
                real, imag = ((real - imag) * c, (real + imag) * c) if sign > 0 else ((real + imag) * c, (imag - real) * c)
            elif 8 * j == 3 * count:
                real, imag = ((real + imag) * c, (imag - real) * c) if sign > 0 else ((real - imag) * c, (real + imag) * c)
            else:
                real, imag = real * c - imag * s, real * s + imag * c
        low.append((even[j][0] + real, even[j][1] + imag))
        high.append((even[j][0] - real, even[j][1] - imag))
    return low + high


def turned(pair, cosine, sine):
    real, imag = pair
    return real * cosine - imag * sine, imag * cosine + real * sine


def scaled(pair, factor):
    return turned(pair, *factor)


def powers_of(root):
    powers = [None, root]
    for v in range(2, RADIX):
        powers.append(turned(powers[v // 2], *powers[v - v // 2]))
    return powers


def transform_kernel(
    taken_ref, taps_ref, forward, cos_ref, sin_ref, inverse, out_ref,
    result_ref, packed, inner, flipped, high_ref, low_ref, done, sems, edges,
):
    devices, tokens, block = done.shape
    half = cos_ref.shape[0]
    lane = [pl.ds(v * block, block) for v in range(RADIX)]
    edge = tokens + 2 * half

    edges[:EDGE] = jnp.zeros((EDGE, block), jnp.float32)
    for q in range(devices):
        edges[pl.ds((q + 1) * EDGE, EDGE)] = taken_ref[q, pl.ds(edge, EDGE), :].astype(jnp.float32)

    def ends(index, own):
        return edges[pl.ds(index + EDGE * own, devices, stride=EDGE), :]

    def first_rows(which):
        taps = taps_ref[which]
        base = 2 * (which - 1)
        now, after = ends(base, 1), ends(base + 1, 1)
        older, newer = ends(base + 4, 0), ends(base + 5, 0)
        return (
            taps[0:1] * now + taps[1:2] * newer + taps[2:3] * older,
            taps[0:1] * after + taps[1:2] * now + taps[2:3] * newer,
        )

    key_rows, value_rows = first_rows(1), first_rows(2)
    first_row, second_row = key_rows[0] * value_rows[0], key_rows[1] * value_rows[1]

    def tokens_of(q):
        top = taken_ref[q, pl.ds(0, ROWS), :].astype(jnp.float32)
        index = lax.broadcasted_iota(jnp.int32, top.shape, 0)
        top = jnp.where(index == 0, first_row[q : q + 1], jnp.where(index == 1, second_row[q : q + 1], top))
        return jnp.concatenate(
            [top.astype(jnp.bfloat16), taken_ref[q, pl.ds(ROWS, tokens - ROWS), :]], axis=0
        )

    def spectrum_rows(start, imag):
        return pl.ds(tokens + start // GROUP * 2 * GROUP + start % GROUP + imag * GROUP, ROWS)

    part = half // RADIX
    matrix = gather_rows(half, RADIX)
    for k in range(0, RADIX, 2):
        slabs = [tokens_of(2 * k + q) for q in range(4)]
        both = exact_rows(
            matrix, jnp.concatenate(slabs[:2], axis=0), jnp.concatenate(slabs[2:], axis=0)
        )
        for v in range(RADIX):
            rows = both[v * part : (v + 1) * part]
            packed[pl.ds(k * part, part), lane[v]] = rows[:, :block]
            packed[pl.ds((k + 1) * part, part), lane[v]] = rows[:, block:]

    row = lax.broadcasted_iota(jnp.int32, (half, half), 0)
    column = lax.broadcasted_iota(jnp.int32, (half, half), 1)
    flip = jnp.where(row + column == half, 1.0, 0.0).astype(jnp.bfloat16)
    for j in range(RADIX):
        source = 2 * RADIX - 1 - 2 * j
        right = jnp.concatenate(
            [
                jnp.concatenate(
                    [
                        taken_ref[source, pl.ds(tokens + (2 * g + imag) * GROUP, GROUP), :]
                        for g in range(half // GROUP)
                    ],
                    axis=0,
                )
                for imag in range(2)
            ],
            axis=1,
        )
        flipped[j] = jnp.dot(flip, right, preferred_element_type=jnp.float32).astype(jnp.bfloat16)

    wide = 2 * block
    for v in range(0, RADIX, 2):
        lanes = pl.ds(v * block, wide)
        right = packed[:, lanes]
        inner[:, lanes] = jnp.dot(forward[...], right, preferred_element_type=jnp.float32)

    def products(rows, start, parts):
        parts = butterfly(parts, -1)
        result = []
        for j in range(RADIX):
            real = taken_ref[2 * j, spectrum_rows(start, 0), :].astype(jnp.float32)
            imag = taken_ref[2 * j, spectrum_rows(start, 1), :].astype(jnp.float32)
            mirror = flipped[j, rows, :].astype(jnp.float32)
            result.append(scaled(parts[j], (real + mirror[:, :block], imag - mirror[:, block:])))
        return butterfly(result, 1)

    def middle(start, first):
        rows = pl.ds(start, ROWS)
        rows_imag = pl.ds(start + half, ROWS)
        top = lax.broadcasted_iota(jnp.int32, (ROWS, block), 0) == 0
        powers = powers_of((cos_ref[rows, :], sin_ref[rows, :]))
        parts, tops = [], []
        for v in range(RADIX):
            real, imag = inner[rows, lane[v]], -inner[rows_imag, lane[v]]
            if first:
                tops.append(-imag)
                imag = jnp.where(top, 0.0, imag)
            if v:
                cosine, sine = powers[v]
                real, imag = turned((real, imag), cosine, -sine)
            parts.append((real, imag))
        parts = products(rows, start, parts)
        if first:
            angles = [math.pi * v / RADIX for v in range(RADIX)]
            nyquist = [(t * math.cos(a), t * -math.sin(a)) for t, a in zip(tops, angles)]
            nyquist = butterfly(nyquist, -1)
            nyquist = [
                scaled(
                    nyquist[j],
                    (
                        taken_ref[2 * j + 1, spectrum_rows(0, 0), :].astype(jnp.float32),
                        taken_ref[2 * j + 1, spectrum_rows(0, 1), :].astype(jnp.float32),
                    ),
                )
                for j in range(RADIX)
            ]
            nyquist = butterfly(nyquist, 1)
            tops = [n[0] * math.cos(a) - n[1] * math.sin(a) for n, a in zip(nyquist, angles)]
        for v in range(RADIX):
            real, imag = parts[v]
            if v:
                real, imag = turned((real, imag), *powers[v])
            imag = jnp.where(top, tops[v], -imag) if first else -imag
            high_ref[rows, lane[v]], low_ref[rows, lane[v]] = split(real)
            high_ref[rows_imag, lane[v]], low_ref[rows_imag, lane[v]] = split(imag)

    middle(0, True)

    @pl.loop(1, half // ROWS)
    def _(i):
        middle(pl.multiple_of(i * ROWS, ROWS), False)

    for v in range(0, RADIX, 2):
        lanes = pl.ds(v * block, wide)
        right = high_ref[:, lanes]
        result = (
            jnp.dot(inverse[...], right, preferred_element_type=jnp.float32)
            + jnp.dot(inverse[...], low_ref[:, lanes], preferred_element_type=jnp.float32)
        ) * (0.5 / (devices * tokens))
        result_ref[:, lanes] = result.astype(jnp.bfloat16)

    matrix = gather_rows(half, RADIX, invert=True)
    copies = []
    for k in range(0, RADIX, 2):
        slabs = [
            jnp.concatenate([result_ref[pl.ds(p * part, part), lane[v]] for v in range(RADIX)], axis=0)
            for p in (k, k + 1)
        ]
        both = exact_rows(matrix, *slabs)
        for q in range(4):
            done[2 * k + q] = both[(q % 2) * tokens : (q % 2 + 1) * tokens, (q // 2) * block : (q // 2 + 1) * block]
        copies.append(
            pltpu.make_async_copy(
                done.at[pl.ds(2 * k, 4)], out_ref.at[pl.ds(2 * k, 4)], sems.at[k // 2]
            )
        )
        copies[-1].start()
    for copy in copies:
        copy.wait()


def angles_of(shape, rows, columns, order):
    index = lax.broadcasted_iota(jnp.int32, shape, rows) * lax.broadcasted_iota(jnp.int32, shape, columns)
    return (2.0 * math.pi / order) * (index & (order - 1)).astype(jnp.float32)


def tables_kernel(forward, cos_ref, sin_ref, inverse):
    depth = forward.shape[1]
    half, block = cos_ref.shape
    order = 2 * RADIX * half

    def alternating(shape, dim):
        return (1 - 2 * (lax.broadcasted_iota(jnp.int32, shape, dim) & 1)).astype(jnp.float32)

    def first(shape, dim):
        return lax.broadcasted_iota(jnp.int32, shape, dim) == 0

    shape = (half, depth)
    angle = angles_of(shape, 0, 1, 2 * half)
    forward[:half] = jnp.cos(angle).astype(jnp.bfloat16)
    sine = jnp.where(first(shape, 0), alternating(shape, 1), jnp.sin(angle))
    forward[half:] = sine.astype(jnp.bfloat16)
    shape = (depth, half)
    angle = angles_of(shape, 0, 1, 2 * half)
    inverse[:, :half] = jnp.cos(angle).astype(jnp.bfloat16)
    sine = jnp.where(first(shape, 1), alternating(shape, 0), jnp.sin(angle))
    inverse[:, half:] = sine.astype(jnp.bfloat16)

    step = lax.broadcasted_iota(jnp.int32, (half, block), 0).astype(jnp.float32)
    angle = (2.0 * math.pi / order) * step
    cos_ref[...] = jnp.cos(angle)
    sin_ref[...] = jnp.sin(angle)


def local_tables(length, block):
    half, depth = length // RADIX, length // RADIX
    whole = pl.BlockSpec(memory_space=pltpu.VMEM)
    forward = jax.ShapeDtypeStruct((2 * half, depth), jnp.bfloat16)
    inverse = jax.ShapeDtypeStruct((depth, 2 * half), jnp.bfloat16)
    twiddle = jax.ShapeDtypeStruct((half, block), jnp.float32)
    return pl.pallas_call(
        tables_kernel,
        out_shape=(forward, twiddle, twiddle, inverse),
        out_specs=(whole,) * 4,
        compiler_params=pltpu.CompilerParams(vmem_limit_bytes=16 * 2**20),
        cost_estimate=pl.CostEstimate(
            flops=200 * RADIX * half * block, bytes_accessed=8 * RADIX * half * block, transcendentals=0
        ),
    )()


def local_transform(taken, taps, tables, tokens):
    devices, _, block = taken.shape
    length = devices * tokens
    half, depth = length // RADIX, length // RADIX
    flops = 3 * 2 * 2 * half * depth * RADIX * block
    whole, remote = pl.BlockSpec(memory_space=pltpu.VMEM), pl.BlockSpec(memory_space=pltpu.HBM)
    wide = RADIX * block
    return pl.pallas_call(
        transform_kernel,
        out_shape=pltpu.HBM((devices, tokens, block), jnp.bfloat16),
        in_specs=[whole] * 6,
        out_specs=remote,
        scratch_shapes=[
            pltpu.VMEM((depth, wide), jnp.bfloat16),
            pltpu.VMEM((depth, wide), jnp.bfloat16),
            pltpu.VMEM((2 * half, wide), jnp.float32),
            pltpu.VMEM((RADIX, half, 2 * block), jnp.bfloat16),
            pltpu.VMEM((2 * half, wide), jnp.bfloat16),
            pltpu.VMEM((2 * half, wide), jnp.bfloat16),
            pltpu.VMEM((devices, tokens, block), jnp.bfloat16),
            pltpu.SemaphoreType.DMA((RADIX // 2,)),
            pltpu.VMEM(((devices + 1) * EDGE, block), jnp.float32),
        ],
        compiler_params=pltpu.CompilerParams(vmem_limit_bytes=20 * 2**20),
        cost_estimate=pl.CostEstimate(flops=flops, bytes_accessed=taken.size * 2, transcendentals=0),
    )(taken, taps, *tables)


def sum_shares(share, axis):
    count = lax.axis_size(axis)
    rank = lax.axis_index(axis)
    columns = share.shape[1] // count
    total = lax.dynamic_slice_in_dim(share, rank * columns, columns, axis=1)
    for step in range(1, count):
        piece = lax.dynamic_slice_in_dim(share, (rank + step) % count * columns, columns, axis=1)
        pairs = [(i, (i + step) % count) for i in range(count)]
        total = total + lax.ppermute(piece.astype(jnp.bfloat16), axis, pairs).astype(jnp.float32)
    return total


def fused_shards(query, key_in, value, short_taps, skip_gain, filter_spectrum, out_weight):
    devices = lax.axis_size("ctx")
    tokens, channels = query.shape
    block = channels // devices
    sent = prepared(key_in, value, short_taps, filter_spectrum, devices)
    taken = lax.all_to_all(sent, "ctx", split_axis=0, concat_axis=0, tiled=True)
    tails = own_tails(query, key_in, value)
    tails = shifted_in(tails, "ctx")
    gate_signal, direct = gates(query, key_in, value, tails, short_taps, skip_gain)
    own_taps = lax.dynamic_slice_in_dim(short_taps, lax.axis_index("ctx") * block, block, axis=2)
    tables = local_tables(tokens * devices, block)
    convolved = local_transform(taken, own_taps, tables, tokens)
    convolved = lax.all_to_all(convolved, "ctx", split_axis=0, concat_axis=0, tiled=True)
    return projected(convolved, gate_signal, direct, out_weight)


def shards(query, key_in, value, short_taps, skip_gain, filter_spectrum, out_weight):
    devices = lax.axis_size("ctx")
    tokens, channels = query.shape
    length, block = tokens * devices, channels // devices
    if block == LANES and devices == 2 * RADIX and lax.axis_size("tp") == 2:
        return fused_shards(query, key_in, value, short_taps, skip_gain, filter_spectrum, out_weight)
    tails = shifted_in(jnp.concatenate([query[-2:], key_in[-2:], value[-2:]], axis=0), "ctx")
    gate_signal = causal_filter(query, tails[0:2], short_taps[0])
    mixed_in = causal_filter(key_in, tails[2:4], short_taps[1]) * causal_filter(
        value, tails[4:6], short_taps[2]
    )
    own_signal = mixed_in.astype(jnp.bfloat16).reshape(tokens, devices, block).transpose(1, 0, 2)
    own_spectrum = (
        filter_spectrum.astype(jnp.bfloat16)
        .reshape(tokens, 2, 2, devices, block)
        .transpose(3, 2, 0, 1, 4)
        .reshape(devices, 4 * tokens, block)
    )
    sent = jnp.concatenate([own_signal, own_spectrum], axis=1)
    taken = lax.all_to_all(sent, "ctx", split_axis=0, concat_axis=0, tiled=True)
    signal = taken[:, :tokens].reshape(length, block)
    spectrum_real = taken[:, tokens : 3 * tokens].reshape(2 * length, block)
    spectrum_imag = taken[:, 3 * tokens :].reshape(2 * length, block)
    convolved = long_filter(signal, spectrum_real, spectrum_imag).astype(jnp.bfloat16)
    convolved = lax.all_to_all(
        convolved.reshape(devices, tokens, block), "ctx", split_axis=0, concat_axis=0, tiled=True
    )
    convolved = convolved.transpose(1, 0, 2).reshape(tokens, channels).astype(jnp.float32)
    gated = (gate_signal * (convolved + skip_gain * mixed_in)).astype(jnp.bfloat16)
    share = jnp.dot(gated, out_weight, preferred_element_type=jnp.float32)
    return sum_shares(share, "tp").astype(jnp.bfloat16)


def solution(mesh):
    return jax.shard_map(
        shards,
        mesh=mesh,
        in_specs=(
            P("ctx", "tp"),
            P("ctx", "tp"),
            P("ctx", "tp"),
            P(None, None, "tp"),
            P("tp"),
            P("ctx", None, None, "tp"),
            P("tp", None),
        ),
        out_specs=P("ctx", "tp"),
        check_vma=False,
    )
```

profile of v0, /device:TPU:0, one launch (start us, length us, event | category | flops | bytes accessed | tf_op | source)
XLA Modules:
  0.0 115.2 jit_solution(15022404714709815107)
XLA Ops:
  0.0 4.1 %shard_map.73 = bf16[16,648,128]{2,1,0:T(8,128)(2,1)} custom-call(f32[8192,128]{1,0:T(8,128)} %bitcast.6, bf16[128,2048]{1,0:T(8,128)(2,1)} %refs_1_.1, bf16[128,2048]{1,0:T(8,128)(2,1)} %refs_2_.1, f32[3,3,2048]{2,1,0:T(4,128)} %refs_3_.1), custom_call_target="tpu_custom_call" | custom-call | bytes 6291456 | tf_op jit(solution)/shard_map/pallas_call | solution.py:213
  4.1 7.4 %all-to-all-start = ((bf16[16,648,128]{2,1,0:T(8,128)(2,1)}), bf16[16,648,128]{2,1,0:T(8,128)(2,1)S(1)}, u32[]{:S(2)}, u32[]{:S(2)}) async-start(bf16[16,648,128]{2,1,0:T(8,128)(2,1)} %shard_map.73), calls=%async_computation | async-start | bytes 5308416 | tf_op jit(solution)/shard_map/all_to_all | solution.py:660
  11.6 1.5 %shard_map.74 = (bf16[512,256]{1,0:T(8,128)(2,1)S(1)}, f32[256,128]{1,0:T(8,128)S(1)}, f32[256,128]{1,0:T(8,128)S(1)}, bf16[256,512]{1,0:T(8,128)(2,1)S(1)}) custom-call(), custom_call_target="tpu_custom_call" | custom-call | flops 52428800 | bytes 2097152 | tf_op jit(solution)/shard_map/pallas_call | solution.py:604
  13.1 0.7 constant_dynamic-slice_fusion.taps_ref
  13.8 48.4 %all-to-all-done.taken_ref = bf16[16,648,128]{2,1,0:T(8,128)(2,1)S(1)} async-done(((bf16[16,648,128]{2,1,0:T(8,128)(2,1)}), bf16[16,648,128]{2,1,0:T(8,128)(2,1)S(1)}, u32[]{:S(2)}, u32[]{:S(2)}) %all-to-all-start) | async-done | bytes 2654240 | tf_op jit(solution)/shard_map/all_to_all | solution.py:660
  62.2 4.5 %shard_map.75 = bf16[16,128,128]{2,1,0:T(8,128)(2,1)} custom-call(bf16[16,648,128]{2,1,0:T(8,128)(2,1)S(1)} %all-to-all-done.taken_ref, f32[3,3,128]{2,1,0:T(4,128)S(1)} %constant_dynamic-slice_fusion.taps_ref, bf16[512,256]{1,0:T(8,128)(2,1)S(1)} %get-tuple-element.13.forward, f32[256,128]{1,0:T(8,128)S(1)} %get-tuple-element.14.cos_ref, ...), custom_call_target="tpu_custom_call" | custom-call | flops 805306368 | bytes 2654208 | tf_op jit(solution)/shard_map/pallas_call | solution.py:622
  66.8 13.5 %all-to-all-start.1 = ((bf16[16,128,128]{2,1,0:T(8,128)(2,1)}), bf16[16,128,128]{2,1,0:T(8,128)(2,1)S(1)}, u32[]{:S(2)}, u32[]{:S(2)}) async-start(bf16[16,128,128]{2,1,0:T(8,128)(2,1)} %shard_map.75), calls=%async_computation.1 | async-start | bytes 1048576 | tf_op jit(solution)/shard_map/all_to_all | solution.py:667
  80.2 0.9 shard_map.76
  81.2 2.3 %collective-permute-start = (bf16[6,2048]{1,0:T(8,128)(2,1)S(1)}, bf16[6,2048]{1,0:T(8,128)(2,1)S(1)}, u32[]{:S(2)}, u32[]{:S(2)}) collective-permute-start(bf16[6,2048]{1,0:T(8,128)(2,1)S(1)} %shard_map.76), channel_id=1, source_target_pairs={{0,2},{2,4},{4,6},{6,8},{8,10},{10,12},{12,14},{14,16},{16,18},{18... | collective-permute-start | bytes 73736 | tf_op jit(solution)/shard_map/ppermute | solution.py:23
  83.5 0.8 collective-permute-done.tails_ref
  84.3 2.6 %shard_map.77 = (f32[128,2048]{1,0:T(8,128)S(1)}, f32[128,2048]{1,0:T(8,128)S(1)}) custom-call(bf16[6,2048]{1,0:T(8,128)(2,1)S(1)} %collective-permute-done.tails_ref, bf16[128,2048]{1,0:T(8,128)(2,1)} %refs_0_.1, bf16[128,2048]{1,0:T(8,128)(2,1)} %refs_1_.1, bf16[128,2048]{1,0:T(8,128)(2,1)} %refs_2_.1, f32[3,3,2048]{2,1,0:T(4,128)} %refs_3_.1, ...), custom_call_target="tpu_custom_call" | custom-call | flops 5242880 | bytes 3670016 | tf_op jit(solution)/shard_map/pallas_call | solution.py:257
  86.9 7.6 %all-to-all-done.1.conv_ref = bf16[16,128,128]{2,1,0:T(8,128)(2,1)S(1)} async-done(((bf16[16,128,128]{2,1,0:T(8,128)(2,1)}), bf16[16,128,128]{2,1,0:T(8,128)(2,1)S(1)}, u32[]{:S(2)}, u32[]{:S(2)}) %all-to-all-start.1) | async-done | bytes 524320 | tf_op jit(solution)/shard_map/all_to_all | solution.py:667
  94.5 2.4 %shard_map.78 = (bf16[128,2048]{1,0:T(8,128)(2,1)S(1)}, bf16[128,768]{1,0:T(8,128)(2,1)S(1)}) custom-call(bf16[16,128,128]{2,1,0:T(8,128)(2,1)S(1)} %all-to-all-done.1.conv_ref, f32[128,2048]{1,0:T(8,128)S(1)} %get-tuple-element.17.gate_ref, f32[128,2048]{1,0:T(8,128)S(1)} %get-tuple-element.18.direct_ref, bf16[2048,4096]{1,0:T(8,128)(2,1)} %weight_ref.5), custom_call_target="tpu_custom_call" | custom-call | flops 402653184 | bytes 3145728 | tf_op jit(solution)/shard_map/pallas_call | solution.py:324
  97.0 3.3 %shard_map.80 = bf16[128,1280]{1,0:T(8,128)(2,1)S(1)} custom-call(bf16[128,2048]{1,0:T(8,128)(2,1)S(1)} %get-tuple-element.19.gated_ref, bf16[2048,4096]{1,0:T(8,128)(2,1)} %weight_ref.5), custom_call_target="tpu_custom_call" | custom-call | flops 671088640 | bytes 5242880 | tf_op jit(solution)/shard_map/pallas_call | solution.py:324
  100.3 1.6 %collective-permute-start.2 = (bf16[128,1280]{1,0:T(8,128)(2,1)S(1)}, bf16[128,1280]{1,0:T(8,128)(2,1)S(1)}, u32[]{:S(2)}, u32[]{:S(2)}) collective-permute-start(bf16[128,1280]{1,0:T(8,128)(2,1)S(1)} %shard_map.80), channel_id=1, source_target_pairs={{0,1},{1,0},{2,3},{3,2},{4,5},{5,4},{6,7},{7,6},{8,9},{9,8},{10,11... | collective-permute-start | bytes 983048 | tf_op jit(solution)/shard_map/ppermute | solution.py:355
  101.8 0.5 collective-permute-start.1
  102.4 4.0 %shard_map.79 = f32[128,2048]{1,0:T(8,128)S(1)} custom-call(bf16[128,2048]{1,0:T(8,128)(2,1)S(1)} %get-tuple-element.19.gated_ref, bf16[2048,4096]{1,0:T(8,128)(2,1)} %weight_ref.5), custom_call_target="tpu_custom_call" | custom-call | flops 1073741824 | bytes 8388608 | tf_op jit(solution)/shard_map/pallas_call | solution.py:324
  106.4 7.9 %collective-permute-done.1 = bf16[128,768]{1,0:T(8,128)(2,1)S(1)} collective-permute-done((bf16[128,768]{1,0:T(8,128)(2,1)S(1)}, bf16[128,768]{1,0:T(8,128)(2,1)S(1)}, u32[]{:S(2)}, u32[]{:S(2)}) %collective-permute-start.1) | collective-permute-done | bytes 196640 | tf_op jit(solution)/shard_map/ppermute | solution.py:355
  114.3 0.0 collective-permute-done.2
  114.3 0.9 add_convert_fusion
Async XLA Ops:
  4.1 58.1 %all-to-all-start = ((bf16[16,648,128]{2,1,0:T(8,128)(2,1)}), bf16[16,648,128]{2,1,0:T(8,128)(2,1)S(1)}, u32[]{:S(2)}, u32[]{:S(2)}) async-start(bf16[16,648,128]{2,1,0:T(8,128)(2,1)} %shard_map.73), calls=%async_computation | async-start | bytes 5308416 | tf_op jit(solution)/shard_map/all_to_all | solution.py:660
  66.8 27.7 %all-to-all-start.1 = ((bf16[16,128,128]{2,1,0:T(8,128)(2,1)}), bf16[16,128,128]{2,1,0:T(8,128)(2,1)S(1)}, u32[]{:S(2)}, u32[]{:S(2)}) async-start(bf16[16,128,128]{2,1,0:T(8,128)(2,1)} %shard_map.75), calls=%async_computation.1 | async-start | bytes 1048576 | tf_op jit(solution)/shard_map/all_to_all | solution.py:667
  81.2 3.2 %collective-permute-start = (bf16[6,2048]{1,0:T(8,128)(2,1)S(1)}, bf16[6,2048]{1,0:T(8,128)(2,1)S(1)}, u32[]{:S(2)}, u32[]{:S(2)}) collective-permute-start(bf16[6,2048]{1,0:T(8,128)(2,1)S(1)} %shard_map.76), channel_id=1, source_target_pairs={{0,2},{2,4},{4,6},{6,8},{8,10},{10,12},{12,14},{14,16},{16,18},{18... | collective-permute-start | bytes 73736 | tf_op jit(solution)/shard_map/ppermute | solution.py:23
  100.3 14.0 %collective-permute-start.2 = (bf16[128,1280]{1,0:T(8,128)(2,1)S(1)}, bf16[128,1280]{1,0:T(8,128)(2,1)S(1)}, u32[]{:S(2)}, u32[]{:S(2)}) collective-permute-start(bf16[128,1280]{1,0:T(8,128)(2,1)S(1)} %shard_map.80), channel_id=1, source_target_pairs={{0,1},{1,0},{2,3},{3,2},{4,5},{5,4},{6,7},{7,6},{8,9},{9,8},{10,11... | collective-permute-start | bytes 983048 | tf_op jit(solution)/shard_map/ppermute | solution.py:355
  101.8 12.5 %collective-permute-start.1 = (bf16[128,768]{1,0:T(8,128)(2,1)S(1)}, bf16[128,768]{1,0:T(8,128)(2,1)S(1)}, u32[]{:S(2)}, u32[]{:S(2)}) collective-permute-start(bf16[128,768]{1,0:T(8,128)(2,1)S(1)} %get-tuple-element.20), channel_id=1, source_target_pairs={{0,1},{1,0},{2,3},{3,2},{4,5},{5,4},{6,7},{7,6},{8,9},{9,8},{10,11... | collective-permute-start | bytes 589832 | tf_op jit(solution)/shard_map/ppermute | solution.py:355
where the time goes:
time: 116 us; the launch traced here: 115 us
  waiting for transfers between devices  64.8 us (56%)
  starting transfers between devices  25.3 us (22%)
  Pallas kernels  23.4 us (20%)
    all_to_all x1, waiting for transfers between devices, fused_shards(): taken = lax.all_to_all(sent, 'ctx', split_axis=0, concat_axis=0, tiled=True)  48.4 us
    all_to_all x1, starting transfers between devices, fused_shards(): lax.all_to_all(convolved, 'ctx', split_axis=0, concat_axis=0, tiled=True)  13.5 us
    pallas_call x3, Pallas kernels, share(): pl.pallas_call(kernel, out_shape=(*extra, jax.ShapeDtypeStruct((tokens, w...  9.73 us
    ppermute x2, waiting for transfers between devices, projected(): arrived.append(lax.ppermute(far, 'tp', swap))  7.94 us
    all_to_all x1, waiting for transfers between devices, fused_shards(): lax.all_to_all(convolved, 'ctx', split_axis=0, concat_axis=0, tiled=True)  7.61 us
    all_to_all x1, starting transfers between devices, fused_shards(): taken = lax.all_to_all(sent, 'ctx', split_axis=0, concat_axis=0, tiled=True)  7.43 us
    pallas_call x1, Pallas kernels, local_transform(): pl.pallas_call(transform_kernel, out_shape=pltpu.HBM((devices, tokens, bl...  4.54 us
    pallas_call x1, Pallas kernels, prepared(): pl.pallas_call(prepare_kernel, out_shape=pltpu.HBM((devices, rows, block)...  4.11 us
  transfers between devices with their start and end apart: 5, of which 4 were waited for; matrix products, arithmetic and copies ran while one was open for 1% of the time, Pallas kernels for 8%

commit v1 on v0

--- a/solution.py
+++ b/solution.py
@@ -12,9 +12,9 @@
 RADIX = 8
 ROWS = 16
 LANES = 128
-FAR_CHUNKS = (768, 1280)
+FAR_CHUNKS = (512, 768, 768)
 STEP = 256
-GROUP = 128
+GROUP = 64
 EDGE = 8
 
 
@@ -167,13 +167,20 @@
     for load in loads[:3]:
         load.wait()
     edge = tokens + 2 * GROUP * groups
-    for j in range(devices):
+    order = gather_rows(tokens, RADIX)
+
+    def mixed(j):
         lanes = pl.ds(j * block, block)
         k, v = key[:, lanes].astype(jnp.float32), value[:, lanes].astype(jnp.float32)
-        mixed = unshifted(k, taps[1, :, lanes]) * unshifted(v, taps[2, :, lanes])
-        staged[j, pl.ds(0, tokens), :] = mixed.astype(jnp.bfloat16)
         ends = jnp.concatenate([k[:2], v[:2], k[tokens - 2 :], v[tokens - 2 :]], axis=0)
         staged[j, pl.ds(edge, EDGE), :] = ends.astype(jnp.bfloat16)
+        product = unshifted(k, taps[1, :, lanes]) * unshifted(v, taps[2, :, lanes])
+        return product.astype(jnp.bfloat16)
+
+    for j in range(0, devices, 2):
+        both = exact_rows(order, mixed(j), mixed(j + 1))
+        staged[j, pl.ds(0, tokens), :] = both[:, :block]
+        staged[j + 1, pl.ds(0, tokens), :] = both[:, block:]
     store(0, tokens)
     store(edge, EDGE)
 
@@ -428,28 +435,21 @@
     key_rows, value_rows = first_rows(1), first_rows(2)
     first_row, second_row = key_rows[0] * value_rows[0], key_rows[1] * value_rows[1]
 
-    def tokens_of(q):
-        top = taken_ref[q, pl.ds(0, ROWS), :].astype(jnp.float32)
-        index = lax.broadcasted_iota(jnp.int32, top.shape, 0)
-        top = jnp.where(index == 0, first_row[q : q + 1], jnp.where(index == 1, second_row[q : q + 1], top))
-        return jnp.concatenate(
-            [top.astype(jnp.bfloat16), taken_ref[q, pl.ds(ROWS, tokens - ROWS), :]], axis=0
-        )
+    def tokens_of(q, v):
+        rows = taken_ref[q, pl.ds(v * ROWS, ROWS), :]
+        if v > 1:
+            return rows
+        top = lax.broadcasted_iota(jnp.int32, rows.shape, 0) == 0
+        right = (first_row, second_row)[v][q : q + 1]
+        return jnp.where(top, right, rows.astype(jnp.float32)).astype(jnp.bfloat16)
 
     def spectrum_rows(start, imag):
         return pl.ds(tokens + start // GROUP * 2 * GROUP + start % GROUP + imag * GROUP, ROWS)
 
     part = half // RADIX
-    matrix = gather_rows(half, RADIX)
-    for k in range(0, RADIX, 2):
-        slabs = [tokens_of(2 * k + q) for q in range(4)]
-        both = exact_rows(
-            matrix, jnp.concatenate(slabs[:2], axis=0), jnp.concatenate(slabs[2:], axis=0)
-        )
+    for q in range(devices):
         for v in range(RADIX):
-            rows = both[v * part : (v + 1) * part]
-            packed[pl.ds(k * part, part), lane[v]] = rows[:, :block]
-            packed[pl.ds((k + 1) * part, part), lane[v]] = rows[:, block:]
+            packed[pl.ds(q * ROWS, ROWS), lane[v]] = tokens_of(q, v)
 
     row = lax.broadcasted_iota(jnp.int32, (half, half), 0)
     column = lax.broadcasted_iota(jnp.int32, (half, half), 1)
@@ -672,7 +672,7 @@
     devices = lax.axis_size("ctx")
     tokens, channels = query.shape
     length, block = tokens * devices, channels // devices
-    if block == LANES and devices == 2 * RADIX and lax.axis_size("tp") == 2:
+    if block == LANES and devices == 2 * RADIX and tokens == ROWS * RADIX and lax.axis_size("tp") == 2:
         return fused_shards(query, key_in, value, short_taps, skip_gain, filter_spectrum, out_weight)
     tails = shifted_in(jnp.concatenate([query[-2:], key_in[-2:], value[-2:]], axis=0), "ctx")
     gate_signal = causal_filter(query, tails[0:2], short_taps[0])

time: 116 us -> 117 us (level)
  Pallas kernels: 23.4 us -> 25 us
  starting transfers between devices: 25.3 us -> 26.8 us
  waiting for transfers between devices: 64.8 us -> 63.3 us
    ppermute x2 -> x3, starting transfers between devices: 2.09 us -> 3.58 us  [projected(): arrived.append(lax.ppermute(far, 'tp', swap))]
    ppermute x2 -> x3, waiting for transfers between devices: 7.94 us -> 6.46 us  [projected(): arrived.append(lax.ppermute(far, 'tp', swap))]
    pallas_call x3 -> x4, Pallas kernels: 9.73 us -> 11 us  [share(): pl.pallas_call(kernel, out_shape=(*extra, jax.ShapeDtypeStruct((tokens, w...]
  transfers between devices with their start and end apart: 5 -> 6, of which waited for: 4 -> 4; matrix products, arithmetic and copies ran while one was open for 1% -> 1% of each run, Pallas kernels for 8% -> 8%
where the time goes in v1:
time: 117 us
  waiting for transfers between devices  63.3 us (54%)
  starting transfers between devices  26.8 us (23%)
  Pallas kernels  25 us (21%)
    all_to_all x1, waiting for transfers between devices, fused_shards(): taken = lax.all_to_all(sent, 'ctx', split_axis=0, concat_axis=0, tiled=True)  48.4 us
    all_to_all x1, starting transfers between devices, fused_shards(): lax.all_to_all(convolved, 'ctx', split_axis=0, concat_axis=0, tiled=True)  13.5 us
    pallas_call x4, Pallas kernels, share(): pl.pallas_call(kernel, out_shape=(*extra, jax.ShapeDtypeStruct((tokens, w...  11 us
    all_to_all x1, waiting for transfers between devices, fused_shards(): lax.all_to_all(convolved, 'ctx', split_axis=0, concat_axis=0, tiled=True)  7.61 us
    all_to_all x1, starting transfers between devices, fused_shards(): taken = lax.all_to_all(sent, 'ctx', split_axis=0, concat_axis=0, tiled=True)  7.43 us
    ppermute x3, waiting for transfers between devices, projected(): arrived.append(lax.ppermute(far, 'tp', swap))  6.46 us
    pallas_call x1, Pallas kernels, prepared(): pl.pallas_call(prepare_kernel, out_shape=pltpu.HBM((devices, rows, block)...  4.6 us
    pallas_call x1, Pallas kernels, local_transform(): pl.pallas_call(transform_kernel, out_shape=pltpu.HBM((devices, tokens, bl...  4.36 us
  transfers between devices with their start and end apart: 6, of which 4 were waited for; matrix products, arithmetic and copies ran while one was open for 1% of the time, Pallas kernels for 8%

profile of v1, /device:TPU:0, one launch (start us, length us, event | category | flops | bytes accessed | tf_op | source)
XLA Modules:
  0.0 116.8 jit_solution(14810676123675224460)
XLA Ops:
  0.0 4.6 %shard_map.73 = bf16[16,648,128]{2,1,0:T(8,128)(2,1)} custom-call(f32[8192,128]{1,0:T(8,128)} %bitcast.6, bf16[128,2048]{1,0:T(8,128)(2,1)} %refs_1_.1, bf16[128,2048]{1,0:T(8,128)(2,1)} %refs_2_.1, f32[3,3,2048]{2,1,0:T(4,128)} %refs_3_.1), custom_call_target="tpu_custom_call" | custom-call | bytes 6291456 | tf_op jit(solution)/shard_map/pallas_call | solution.py:220
  4.6 7.4 %all-to-all-start = ((bf16[16,648,128]{2,1,0:T(8,128)(2,1)}), bf16[16,648,128]{2,1,0:T(8,128)(2,1)S(1)}, u32[]{:S(2)}, u32[]{:S(2)}) async-start(bf16[16,648,128]{2,1,0:T(8,128)(2,1)} %shard_map.73), calls=%async_computation | async-start | bytes 5308416 | tf_op jit(solution)/shard_map/all_to_all | solution.py:660
  12.0 1.5 %shard_map.74 = (bf16[512,256]{1,0:T(8,128)(2,1)S(1)}, f32[256,128]{1,0:T(8,128)S(1)}, f32[256,128]{1,0:T(8,128)S(1)}, bf16[256,512]{1,0:T(8,128)(2,1)S(1)}) custom-call(), custom_call_target="tpu_custom_call" | custom-call | flops 52428800 | bytes 2097152 | tf_op jit(solution)/shard_map/pallas_call | solution.py:604
  13.6 0.7 constant_dynamic-slice_fusion.taps_ref
  14.3 48.4 %all-to-all-done.taken_ref = bf16[16,648,128]{2,1,0:T(8,128)(2,1)S(1)} async-done(((bf16[16,648,128]{2,1,0:T(8,128)(2,1)}), bf16[16,648,128]{2,1,0:T(8,128)(2,1)S(1)}, u32[]{:S(2)}, u32[]{:S(2)}) %all-to-all-start) | async-done | bytes 2654240 | tf_op jit(solution)/shard_map/all_to_all | solution.py:660
  62.7 4.4 %shard_map.75 = bf16[16,128,128]{2,1,0:T(8,128)(2,1)} custom-call(bf16[16,648,128]{2,1,0:T(8,128)(2,1)S(1)} %all-to-all-done.taken_ref, f32[3,3,128]{2,1,0:T(4,128)S(1)} %constant_dynamic-slice_fusion.taps_ref, bf16[512,256]{1,0:T(8,128)(2,1)S(1)} %get-tuple-element.13.forward, f32[256,128]{1,0:T(8,128)S(1)} %get-tuple-element.14.cos_ref, ...), custom_call_target="tpu_custom_call" | custom-call | flops 805306368 | bytes 2654208 | tf_op jit(solution)/shard_map/pallas_call | solution.py:622
  67.1 13.5 %all-to-all-start.1 = ((bf16[16,128,128]{2,1,0:T(8,128)(2,1)}), bf16[16,128,128]{2,1,0:T(8,128)(2,1)S(1)}, u32[]{:S(2)}, u32[]{:S(2)}) async-start(bf16[16,128,128]{2,1,0:T(8,128)(2,1)} %shard_map.75), calls=%async_computation.1 | async-start | bytes 1048576 | tf_op jit(solution)/shard_map/all_to_all | solution.py:667
  80.6 0.9 shard_map.76
  81.5 2.3 %collective-permute-start = (bf16[6,2048]{1,0:T(8,128)(2,1)S(1)}, bf16[6,2048]{1,0:T(8,128)(2,1)S(1)}, u32[]{:S(2)}, u32[]{:S(2)}) collective-permute-start(bf16[6,2048]{1,0:T(8,128)(2,1)S(1)} %shard_map.76), channel_id=1, source_target_pairs={{0,2},{2,4},{4,6},{6,8},{8,10},{10,12},{12,14},{14,16},{16,18},{18... | collective-permute-start | bytes 73736 | tf_op jit(solution)/shard_map/ppermute | solution.py:23
  83.8 0.8 collective-permute-done.tails_ref
  84.6 2.6 %shard_map.77 = (f32[128,2048]{1,0:T(8,128)S(1)}, f32[128,2048]{1,0:T(8,128)S(1)}) custom-call(bf16[6,2048]{1,0:T(8,128)(2,1)S(1)} %collective-permute-done.tails_ref, bf16[128,2048]{1,0:T(8,128)(2,1)} %refs_0_.1, bf16[128,2048]{1,0:T(8,128)(2,1)} %refs_1_.1, bf16[128,2048]{1,0:T(8,128)(2,1)} %refs_2_.1, f32[3,3,2048]{2,1,0:T(4,128)} %refs_3_.1, ...), custom_call_target="tpu_custom_call" | custom-call | flops 5242880 | bytes 3670016 | tf_op jit(solution)/shard_map/pallas_call | solution.py:264
  87.2 7.6 %all-to-all-done.1.conv_ref = bf16[16,128,128]{2,1,0:T(8,128)(2,1)S(1)} async-done(((bf16[16,128,128]{2,1,0:T(8,128)(2,1)}), bf16[16,128,128]{2,1,0:T(8,128)(2,1)S(1)}, u32[]{:S(2)}, u32[]{:S(2)}) %all-to-all-start.1) | async-done | bytes 524320 | tf_op jit(solution)/shard_map/all_to_all | solution.py:667
  94.8 2.1 %shard_map.78 = (bf16[128,2048]{1,0:T(8,128)(2,1)S(1)}, bf16[128,512]{1,0:T(8,128)(2,1)S(1)}) custom-call(bf16[16,128,128]{2,1,0:T(8,128)(2,1)S(1)} %all-to-all-done.1.conv_ref, f32[128,2048]{1,0:T(8,128)S(1)} %get-tuple-element.17.gate_ref, f32[128,2048]{1,0:T(8,128)S(1)} %get-tuple-element.18.direct_ref, bf16[2048,4096]{1,0:T(8,128)(2,1)} %weight_ref.7), custom_call_target="tpu_custom_call" | custom-call | flops 268435456 | bytes 2097152 | tf_op jit(solution)/shard_map/pallas_call | solution.py:331
  96.9 2.4 %shard_map.81 = bf16[128,768]{1,0:T(8,128)(2,1)S(1)} custom-call(bf16[128,2048]{1,0:T(8,128)(2,1)S(1)} %get-tuple-element.19.gated_ref, bf16[2048,4096]{1,0:T(8,128)(2,1)} %weight_ref.7), custom_call_target="tpu_custom_call" | custom-call | flops 402653184 | bytes 3145728 | tf_op jit(solution)/shard_map/pallas_call | solution.py:331
  99.4 2.4 %shard_map.80 = bf16[128,768]{1,0:T(8,128)(2,1)S(1)} custom-call(bf16[128,2048]{1,0:T(8,128)(2,1)S(1)} %get-tuple-element.19.gated_ref, bf16[2048,4096]{1,0:T(8,128)(2,1)} %weight_ref.7), custom_call_target="tpu_custom_call" | custom-call | flops 402653184 | bytes 3145728 | tf_op jit(solution)/shard_map/pallas_call | solution.py:331
  101.8 1.6 %collective-permute-start.3 = (bf16[128,768]{1,0:T(8,128)(2,1)S(1)}, bf16[128,768]{1,0:T(8,128)(2,1)S(1)}, u32[]{:S(2)}, u32[]{:S(2)}) collective-permute-start(bf16[128,768]{1,0:T(8,128)(2,1)S(1)} %shard_map.81), channel_id=1, source_target_pairs={{0,1},{1,0},{2,3},{3,2},{4,5},{5,4},{6,7},{7,6},{8,9},{9,8},{10,11... | collective-permute-start | bytes 589832 | tf_op jit(solution)/shard_map/ppermute | solution.py:362
  103.4 0.5 collective-permute-start.2
  103.9 1.5 %collective-permute-start.1 = (bf16[128,512]{1,0:T(8,128)(2,1)S(1)}, bf16[128,512]{1,0:T(8,128)(2,1)S(1)}, u32[]{:S(2)}, u32[]{:S(2)}) collective-permute-start(bf16[128,512]{1,0:T(8,128)(2,1)S(1)} %get-tuple-element.20), channel_id=1, source_target_pairs={{0,1},{1,0},{2,3},{3,2},{4,5},{5,4},{6,7},{7,6},{8,9},{9,8},{10,11... | collective-permute-start | bytes 393224 | tf_op jit(solution)/shard_map/ppermute | solution.py:362
  105.4 4.0 %shard_map.79 = f32[128,2048]{1,0:T(8,128)S(1)} custom-call(bf16[128,2048]{1,0:T(8,128)(2,1)S(1)} %get-tuple-element.19.gated_ref, bf16[2048,4096]{1,0:T(8,128)(2,1)} %weight_ref.7), custom_call_target="tpu_custom_call" | custom-call | flops 1073741824 | bytes 8388608 | tf_op jit(solution)/shard_map/pallas_call | solution.py:331
  109.4 6.5 %collective-permute-done.1 = bf16[128,512]{1,0:T(8,128)(2,1)S(1)} collective-permute-done((bf16[128,512]{1,0:T(8,128)(2,1)S(1)}, bf16[128,512]{1,0:T(8,128)(2,1)S(1)}, u32[]{:S(2)}, u32[]{:S(2)}) %collective-permute-start.1) | collective-permute-done | bytes 131104 | tf_op jit(solution)/shard_map/ppermute | solution.py:362
  115.9 0.0 collective-permute-done.3
  115.9 0.0 collective-permute-done.2
  115.9 0.9 add_convert_fusion
Async XLA Ops:
  4.6 58.1 %all-to-all-start = ((bf16[16,648,128]{2,1,0:T(8,128)(2,1)}), bf16[16,648,128]{2,1,0:T(8,128)(2,1)S(1)}, u32[]{:S(2)}, u32[]{:S(2)}) async-start(bf16[16,648,128]{2,1,0:T(8,128)(2,1)} %shard_map.73), calls=%async_computation | async-start | bytes 5308416 | tf_op jit(solution)/shard_map/all_to_all | solution.py:660
  67.1 27.7 %all-to-all-start.1 = ((bf16[16,128,128]{2,1,0:T(8,128)(2,1)}), bf16[16,128,128]{2,1,0:T(8,128)(2,1)S(1)}, u32[]{:S(2)}, u32[]{:S(2)}) async-start(bf16[16,128,128]{2,1,0:T(8,128)(2,1)} %shard_map.75), calls=%async_computation.1 | async-start | bytes 1048576 | tf_op jit(solution)/shard_map/all_to_all | solution.py:667
  81.5 3.2 %collective-permute-start = (bf16[6,2048]{1,0:T(8,128)(2,1)S(1)}, bf16[6,2048]{1,0:T(8,128)(2,1)S(1)}, u32[]{:S(2)}, u32[]{:S(2)}) collective-permute-start(bf16[6,2048]{1,0:T(8,128)(2,1)S(1)} %shard_map.76), channel_id=1, source_target_pairs={{0,2},{2,4},{4,6},{6,8},{8,10},{10,12},{12,14},{14,16},{16,18},{18... | collective-permute-start | bytes 73736 | tf_op jit(solution)/shard_map/ppermute | solution.py:23
  101.8 14.0 %collective-permute-start.3 = (bf16[128,768]{1,0:T(8,128)(2,1)S(1)}, bf16[128,768]{1,0:T(8,128)(2,1)S(1)}, u32[]{:S(2)}, u32[]{:S(2)}) collective-permute-start(bf16[128,768]{1,0:T(8,128)(2,1)S(1)} %shard_map.81), channel_id=1, source_target_pairs={{0,1},{1,0},{2,3},{3,2},{4,5},{5,4},{6,7},{7,6},{8,9},{9,8},{10,11... | collective-permute-start | bytes 589832 | tf_op jit(solution)/shard_map/ppermute | solution.py:362
  103.4 12.5 %collective-permute-start.2 = (bf16[128,768]{1,0:T(8,128)(2,1)S(1)}, bf16[128,768]{1,0:T(8,128)(2,1)S(1)}, u32[]{:S(2)}, u32[]{:S(2)}) collective-permute-start(bf16[128,768]{1,0:T(8,128)(2,1)S(1)} %shard_map.80), channel_id=1, source_target_pairs={{0,1},{1,0},{2,3},{3,2},{4,5},{5,4},{6,7},{7,6},{8,9},{9,8},{10,11... | collective-permute-start | bytes 589832 | tf_op jit(solution)/shard_map/ppermute | solution.py:362
  103.9 11.9 %collective-permute-start.1 = (bf16[128,512]{1,0:T(8,128)(2,1)S(1)}, bf16[128,512]{1,0:T(8,128)(2,1)S(1)}, u32[]{:S(2)}, u32[]{:S(2)}) collective-permute-start(bf16[128,512]{1,0:T(8,128)(2,1)S(1)} %get-tuple-element.20), channel_id=1, source_target_pairs={{0,1},{1,0},{2,3},{3,2},{4,5},{5,4},{6,7},{7,6},{8,9},{9,8},{10,11... | collective-permute-start | bytes 393224 | tf_op jit(solution)/shard_map/ppermute | solution.py:362
